TPU v7x, 32 devices: a whole 2x2x4 slice. The times are simulated.
32 devices in a mesh: dp: 4 (over y, core), expert: 8 (over z, x).
Axes of the slice: x: 2, y: 2, z: 4, core: 2. Of those that a mesh axis runs over, the one named last changes fastest.
Arguments:
- tokens_in: bfloat16 [32768, 768], P(('dp', 'expert')), may hold values from -6 to 6
- token_ids: int32 [32768], P(('dp', 'expert')), may hold values from 0 to 50303, as said below
- hash_table: int32 [50304], replicated, may hold values from 0 to 7, as said below
- gain_attn: bfloat16 [768], P(('dp', 'expert')), may hold values from 0.25 to 1.75
- gain_ffn: bfloat16 [768], P(('dp', 'expert')), may hold values from 0.25 to 1.75
- w_qkv: bfloat16 [768, 2304], P(('dp', 'expert')), may hold values from -0.21875 to 0.21875
- w_o: bfloat16 [768, 768], P(('dp', 'expert')), may hold values from -1.5 to 1.5
- w_in: bfloat16 [8, 768, 3072], P('expert', None, 'dp'), may hold values from -0.21875 to 0.21875
- w_out: bfloat16 [8, 3072, 768], P('expert', 'dp'), may hold values from -0.109375 to 0.109375
- cotangent: bfloat16 [32768, 768], P(('dp', 'expert')), may hold values from -6 to 6
Outputs:
- block_out: bfloat16 [32768, 768], P(('dp', 'expert'))
- grad_tokens: bfloat16 [32768, 768], P(('dp', 'expert'))
- grad_w_qkv: float32 [768, 2304], P(('dp', 'expert'))
- grad_w_o: float32 [768, 768], P(('dp', 'expert'))
- grad_gain_attn: float32 [768], P(('dp', 'expert'))
- grad_gain_ffn: float32 [768], P(('dp', 'expert'))
- grad_w_in: float32 [8, 768, 3072], P('expert', None, 'dp')
- grad_w_out: float32 [8, 3072, 768], P('expert', 'dp')
Inputs may be any that keep to these rules, and one draw needn't show every extreme that they name: `hash_table`: each of the 8 experts is the value for exactly 6288 ids. `token_ids`: each aligned block of 1024 tokens holds at most 256 tokens that hash_table sends to any one expert, and exactly 256 for one expert, which is the same expert for all blocks of an aligned run of 8192 tokens.
All inputs are finite; a program needn't handle non-finite values.
Results may differ from a plain program's by a relative error of at most 0.013.
Values may be sent and summed in bfloat16 or wider, within the bound.
A program may use at most 256 MiB of HBM per device.

v0:
```python
import jax
import jax.numpy as jnp
from jax import lax
from jax.sharding import PartitionSpec as P

HEADS = 12
SEQ = 1024


EPS = 1e-05
NEG = -1e30
GELU_C = 0.7978845608028654


def gelu_tanh(values):
    return 0.5 * values * (1.0 + jnp.tanh(GELU_C * (values + 0.044715 * values * values * values)))


def gelu_slope(values):
    inner = jnp.tanh(GELU_C * (values + 0.044715 * values * values * values))
    return 0.5 * (1.0 + inner) + 0.5 * values * (1.0 - inner * inner) * GELU_C * (
        1.0 + 3.0 * 0.044715 * values * values
    )


def norm_parts(values):
    centre = jnp.mean(values, axis=-1, keepdims=True)
    shifted = values - centre
    spread = jnp.mean(shifted * shifted, axis=-1, keepdims=True)
    inverse = lax.rsqrt(spread + EPS)
    return (shifted * inverse, inverse)


def norm_grad(upstream, gain, normed, inverse):
    scaled = upstream * gain
    return inverse * (
        scaled
        - jnp.mean(scaled, axis=-1, keepdims=True)
        - normed * jnp.mean(scaled * normed, axis=-1, keepdims=True)
    )


def contract_rows(left, right):
    return lax.dot_general(
        left, right, (((0,), (0,)), ((), ())), preferred_element_type=jnp.float32
    )


def contract_cols(left, right):
    return lax.dot_general(
        left, right, (((1,), (1,)), ((), ())), preferred_element_type=jnp.float32
    )


def attention_weights(gain_attn, gain_ffn, w_qkv, w_o):
    return (
        lax.all_gather(w_qkv, ("dp", "expert"), axis=0, tiled=True),
        lax.all_gather(w_o, ("dp", "expert"), axis=0, tiled=True),
        lax.all_gather(gain_attn, ("dp", "expert"), axis=0, tiled=True),
        lax.all_gather(gain_ffn, ("dp", "expert"), axis=0, tiled=True),
    )


def block_scores(query_block, key_rows, query_start, seq_len):
    scale = query_block.shape[-1] ** (-0.5)
    scores = (
        jnp.einsum("qhd,khd->hqk", query_block, key_rows, preferred_element_type=jnp.float32)
        * scale
    )
    query_pos = query_start + jnp.arange(query_block.shape[0], dtype=jnp.int32)[:, None]
    key_pos = jnp.arange(key_rows.shape[0], dtype=jnp.int32)[None, :]
    same_seq = key_pos // seq_len == query_pos // seq_len
    allowed = same_seq & (key_pos <= query_pos)
    return jnp.where(allowed[None], scores, NEG)


def per_device(
    tokens_in, token_ids, hash_table, gain_attn, gain_ffn, w_qkv, w_o, w_in, w_out, cotangent
):
    tok_rows, model_width = tokens_in.shape
    head_count = HEADS
    head_size = model_width // head_count
    scale = head_size ** (-0.5)
    seq_len = SEQ
    n_expert = lax.axis_size("expert")
    slot_most = 2 * tok_rows // n_expert
    slot_count = n_expert * slot_most
    block_rows = min(512, tok_rows)
    n_blocks = tok_rows // block_rows
    qkv_full, out_full, gain_one, gain_two = attention_weights(gain_attn, gain_ffn, w_qkv, w_o)
    gain_one = gain_one.astype(jnp.float32)
    gain_two = gain_two.astype(jnp.float32)
    inputs = tokens_in.astype(jnp.float32)
    normed_one, inverse_one = norm_parts(inputs)
    act_one = (normed_one * gain_one).astype(jnp.bfloat16)
    qkv = jnp.dot(act_one, qkv_full, preferred_element_type=jnp.float32).astype(jnp.bfloat16)
    query_rows = qkv[:, :model_width].reshape(tok_rows, head_count, head_size)
    key_rows = qkv[:, model_width : 2 * model_width].reshape(tok_rows, head_count, head_size)
    value_rows = qkv[:, 2 * model_width :].reshape(tok_rows, head_count, head_size)
    query_blocks = query_rows.reshape(n_blocks, block_rows, head_count, head_size)
    block_starts = jnp.arange(n_blocks, dtype=jnp.int32) * block_rows

    def forward_block(block_args):
        query_block, query_start = block_args
        scores = block_scores(query_block, key_rows, query_start, seq_len)
        row_max = jnp.max(scores, axis=-1, keepdims=True)
        weights = jnp.exp(scores - row_max)
        row_sum = jnp.sum(weights, axis=-1, keepdims=True)
        prob_low = (weights / row_sum).astype(jnp.bfloat16)
        context = jnp.einsum(
            "hqk,khd->qhd", prob_low, value_rows, preferred_element_type=jnp.float32
        )
        return (
            context.reshape(block_rows, model_width).astype(jnp.bfloat16),
            (row_max + jnp.log(row_sum))[..., 0],
        )

    context, log_total = lax.map(forward_block, (query_blocks, block_starts))
    context = context.reshape(tok_rows, model_width)
    mixed = inputs + jnp.dot(context, out_full, preferred_element_type=jnp.float32)
    normed_two, inverse_two = norm_parts(mixed)
    act_two = (normed_two * gain_two).astype(jnp.bfloat16)
    expert_ids = hash_table[token_ids]
    one_hot = (expert_ids[:, None] == jnp.arange(n_expert, dtype=jnp.int32)[None, :]).astype(
        jnp.int32
    )
    before = jnp.cumsum(one_hot, axis=0) - one_hot
    slot_index = expert_ids * slot_most + jnp.sum(before * one_hot, axis=1)
    send_rows = jnp.zeros((slot_count, model_width), jnp.bfloat16).at[slot_index].set(act_two)
    recv_rows = lax.all_to_all(
        send_rows.reshape(n_expert, slot_most, model_width),
        "expert",
        split_axis=0,
        concat_axis=0,
        tiled=True,
    ).reshape(slot_count, model_width)
    w_in_full, w_out_full = (
        lax.all_gather(w_in, "dp", axis=2, tiled=True),
        lax.all_gather(w_out, "dp", axis=1, tiled=True),
    )
    w_in_full = w_in_full[0]
    w_out_full = w_out_full[0]
    pre_act = jnp.dot(recv_rows, w_in_full, preferred_element_type=jnp.float32)
    hidden = gelu_tanh(pre_act).astype(jnp.bfloat16)
    expert_out = jnp.dot(hidden, w_out_full, preferred_element_type=jnp.float32).astype(
        jnp.bfloat16
    )
    returned = lax.all_to_all(
        expert_out.reshape(n_expert, slot_most, model_width),
        "expert",
        split_axis=0,
        concat_axis=0,
        tiled=True,
    ).reshape(slot_count, model_width)
    branch_out = returned[slot_index]
    block_out = (mixed + branch_out.astype(jnp.float32)).astype(jnp.bfloat16)
    grad_send = jnp.zeros((slot_count, model_width), jnp.bfloat16).at[slot_index].set(cotangent)
    grad_rows = lax.all_to_all(
        grad_send.reshape(n_expert, slot_most, model_width),
        "expert",
        split_axis=0,
        concat_axis=0,
        tiled=True,
    ).reshape(slot_count, model_width)
    pre_again = jnp.dot(recv_rows, w_in_full, preferred_element_type=jnp.float32)
    hidden_again = gelu_tanh(pre_again).astype(jnp.bfloat16)
    grad_out_full = contract_rows(hidden_again, grad_rows)
    grad_hidden = contract_cols(grad_rows, w_out_full)
    grad_pre = (grad_hidden * gelu_slope(pre_again)).astype(jnp.bfloat16)
    grad_in_full = contract_rows(recv_rows, grad_pre)
    grad_act = contract_cols(grad_pre, w_in_full).astype(jnp.bfloat16)
    grad_w_in, grad_w_out = (
        lax.psum_scatter(
            grad_in_full[None].astype(jnp.bfloat16), "dp", scatter_dimension=2, tiled=True
        ).astype(jnp.float32),
        lax.psum_scatter(
            grad_out_full[None].astype(jnp.bfloat16), "dp", scatter_dimension=1, tiled=True
        ).astype(jnp.float32),
    )
    grad_back = lax.all_to_all(
        grad_act.reshape(n_expert, slot_most, model_width),
        "expert",
        split_axis=0,
        concat_axis=0,
        tiled=True,
    ).reshape(slot_count, model_width)
    grad_act_two = grad_back[slot_index].astype(jnp.float32)
    grad_gain_two = jnp.sum(grad_act_two * normed_two, axis=0)
    grad_mixed = cotangent.astype(jnp.float32) + norm_grad(
        grad_act_two, gain_two, normed_two, inverse_two
    )
    grad_branch = grad_mixed.astype(jnp.bfloat16)
    grad_out_proj = contract_rows(context, grad_branch)
    gathered_again = attention_weights(gain_attn, gain_ffn, w_qkv, w_o)
    qkv_back = gathered_again[0]
    out_back = gathered_again[1]
    grad_context = contract_cols(grad_branch, out_back).astype(jnp.bfloat16)
    grad_context = grad_context.reshape(n_blocks, block_rows, head_count, head_size)

    def backward_block(carry, block_args):
        grad_keys, grad_values = carry
        query_block, query_start, log_block, grad_block = block_args
        scores = block_scores(query_block, key_rows, query_start, seq_len)
        probs = jnp.exp(scores - log_block[..., None])
        prob_low = probs.astype(jnp.bfloat16)
        grad_probs = jnp.einsum(
            "qhd,khd->hqk", grad_block, value_rows, preferred_element_type=jnp.float32
        )
        grad_values = grad_values + jnp.einsum(
            "hqk,qhd->khd", prob_low, grad_block, preferred_element_type=jnp.float32
        )
        grad_scores = probs * (grad_probs - jnp.sum(grad_probs * probs, axis=-1, keepdims=True))
        grad_scores = grad_scores.astype(jnp.bfloat16)
        grad_query = (
            jnp.einsum("hqk,khd->qhd", grad_scores, key_rows, preferred_element_type=jnp.float32)
            * scale
        )
        grad_keys = (
            grad_keys
            + jnp.einsum(
                "hqk,qhd->khd", grad_scores, query_block, preferred_element_type=jnp.float32
            )
            * scale
        )
        return ((grad_keys, grad_values), grad_query)

    zero_kv = jnp.zeros((tok_rows, head_count, head_size), jnp.float32)
    (grad_keys, grad_values), grad_query = lax.scan(
        backward_block, (zero_kv, zero_kv), (query_blocks, block_starts, log_total, grad_context)
    )
    grad_qkv = jnp.concatenate(
        [
            grad_query.reshape(tok_rows, model_width),
            grad_keys.reshape(tok_rows, model_width),
            grad_values.reshape(tok_rows, model_width),
        ],
        axis=1,
    )
    grad_qkv = grad_qkv.astype(jnp.bfloat16)
    grad_qkv_proj = contract_rows(act_one, grad_qkv)
    grad_act_one = contract_cols(grad_qkv, qkv_back)
    grad_gain_one = jnp.sum(grad_act_one * normed_one, axis=0)
    grad_tokens = (grad_mixed + norm_grad(grad_act_one, gain_one, normed_one, inverse_one)).astype(
        jnp.bfloat16
    )
    grad_w_qkv, grad_w_o, grad_gain_attn, grad_gain_ffn = (
        lax.psum_scatter(grad_qkv_proj, ("dp", "expert"), scatter_dimension=0, tiled=True),
        lax.psum_scatter(grad_out_proj, ("dp", "expert"), scatter_dimension=0, tiled=True),
        lax.psum_scatter(grad_gain_one, ("dp", "expert"), scatter_dimension=0, tiled=True),
        lax.psum_scatter(grad_gain_two, ("dp", "expert"), scatter_dimension=0, tiled=True),
    )
    return (
        block_out,
        grad_tokens,
        grad_w_qkv,
        grad_w_o,
        grad_gain_attn,
        grad_gain_ffn,
        grad_w_in,
        grad_w_out,
    )


def solution(mesh):
    return jax.shard_map(
        per_device,
        mesh=mesh,
        in_specs=(
            P(("dp", "expert"), None),
            P(("dp", "expert")),
            P(),
            P(("dp", "expert")),
            P(("dp", "expert")),
            P(("dp", "expert"), None),
            P(("dp", "expert"), None),
            P("expert", None, "dp"),
            P("expert", "dp", None),
            P(("dp", "expert"), None),
        ),
        out_specs=(
            P(("dp", "expert"), None),
            P(("dp", "expert"), None),
            P(("dp", "expert"), None),
            P(("dp", "expert"), None),
            P(("dp", "expert")),
            P(("dp", "expert")),
            P("expert", None, "dp"),
            P("expert", "dp", None),
        ),
        check_vma=False,
    )
```

profile of v0, /device:TPU:0, one launch (start us, length us, event | category | flops | bytes accessed | tf_op | source)
XLA Modules:
  0.0 863.5 jit_solution(12311129789460759756)
XLA Ops:
  11.2 42.1 %all-reduce.5 = (bf16[768]{0:T(1024)(128)(2,1)S(1)}, bf16[768]{0:T(1024)(128)(2,1)S(1)}) all-reduce(bf16[768]{0:T(1024)(128)(2,1)S(1)} %dynamic-update-slice, bf16[768]{0:T(1024)(128)(2,1)S(1)} %dynamic-update-slice.1), channel_id=1, replica_groups=mesh['dp'=4,'expert'=8] {'dp','expert'}, use_global_device_ids=true, to_apply=%add | all-reduce | flops 1536 | bytes 6144
  54.5 6.1 gather_fusion
  65.6 8.4 all-gather.5.cloned.1.call-done
  74.0 6.3 convolution_convert_fusion
  82.4 2.6 copy.50
  88.3 3.8 reshape_reshape.3
  93.9 81.7 %while.33 = (s32[]{:T(128)}, bf16[2,512,768]{2,1,0:T(8,128)(2,1)}, f32[2,12,512]{2,1,0:T(8,128)S(1)}, s32[2]{0:T(128)S(1)}, bf16[2,512,12,64]{1,3,2,0:T(8,128)(2...) while((s32[]{:T(128)}, bf16[2,512,768]{2,1,0:T(8,128)(2,1)}, ...), condition=%wide.region_5.6_spmd, body=%wide.region_2.5_spmd.sunk | while | flops 1688086528 | bytes 192651440 | solution.py:118
  95.9 10.8 %fusion.151 = (f32[12,512]{1,0:T(8,128)S(1)}, f32[12,512,1024]{2,1,0:T(8,128)}) fusion(pred[512,1024]{1,0:T(8,128)(4,1)S(1)} %fusion.150, bf16[1024,12,64]{0,2,1:T(8,128)(2,1)S(1)} %get-tuple-element.595, bf16[2,512,12,64]{1,3,2,0:T(8,128)(2,1)S(1)} %get-tuple-element.594, s32[]{:T(128)S(6)} %copy.78), kind=kOutput, calls=%fused_computation.8.clone.1 | convolution fusion | flops 824174592 | bytes 28073988 | tf_op jit(solution)/shard_map/while/body/eval_jaxpr/qhd,khd->hqk/dot_general | solution.py:67
  106.7 12.4 %fusion.152 = f32[12,512]{1,0:T(8,128)S(1)} fusion(f32[12,512,1024]{2,1,0:T(8,128)} %get-tuple-element.558, f32[12,512]{1,0:T(8,128)S(1)} %get-tuple-element.559, pred[512,1024]{1,0:T(8,128)(4,1)S(1)} %fusion.150), kind=kLoop, calls=%fused_computation.9.clone.1 | loop fusion | flops 25159680 | bytes 25739264 | tf_op jit(solution)/shard_map/while/body/eval_jaxpr/reduce_sum | solution.py:108
  119.2 3.1 copy-done.2
  122.3 8.0 fusion.153
  130.3 2.3 copy.69
  136.5 11.1 %fusion.151 = (f32[12,512]{1,0:T(8,128)S(1)}, f32[12,512,1024]{2,1,0:T(8,128)}) fusion(pred[512,1024]{1,0:T(8,128)(4,1)S(1)} %fusion.150, bf16[1024,12,64]{0,2,1:T(8,128)(2,1)S(1)} %get-tuple-element.595, bf16[2,512,12,64]{1,3,2,0:T(8,128)(2,1)S(1)} %get-tuple-element.594, s32[]{:T(128)S(6)} %copy.78), kind=kOutput, calls=%fused_computation.8.clone.1 | convolution fusion | flops 824174592 | bytes 28073988 | tf_op jit(solution)/shard_map/while/body/eval_jaxpr/qhd,khd->hqk/dot_general | solution.py:67
  147.6 12.5 %fusion.152 = f32[12,512]{1,0:T(8,128)S(1)} fusion(f32[12,512,1024]{2,1,0:T(8,128)} %get-tuple-element.558, f32[12,512]{1,0:T(8,128)S(1)} %get-tuple-element.559, pred[512,1024]{1,0:T(8,128)(4,1)S(1)} %fusion.150), kind=kLoop, calls=%fused_computation.9.clone.1 | loop fusion | flops 25159680 | bytes 25739264 | tf_op jit(solution)/shard_map/while/body/eval_jaxpr/reduce_sum | solution.py:108
  160.1 3.2 copy-done.2
  163.3 8.0 fusion.153
  171.3 2.3 copy.69
  175.7 4.9 fusion.109
  183.4 7.6 scatter_custom_fusion
  191.0 4.7 all-to-all-start
  195.6 7.9 scatter_custom_fusion.1
  203.5 63.3 %all-to-all-done = bf16[8,256,768]{2,1,0:T(8,128)(2,1)S(1)} async-done(((bf16[8,256,768]{2,1,0:T(8,128)(2,1)}), bf16[8,256,768]{2,1,0:T(8,128)(2,1)S(1)}, u32[]{:S(2)}, u32[]{:S(2)}) %all-to-all-start) | async-done | bytes 3145760 | tf_op jit(solution)/shard_map/all_to_all | solution.py:130
  266.8 4.5 all-to-all-start.2
  272.3 22.5 %multiply_convert_fusion.1 = (bf16[2048,3072]{1,0:T(8,128)(2,1)}, f32[2048,3072]{1,0:T(8,128)}) fusion(bf16[2048,768]{1,0:T(8,128)(2,1)S(1)} %bitcast.166, bf16[1,768,3072]{2,1,0:T(8,128)(2,1)} %all-gather.9.cloned.1.call-done), kind=kOutput, calls=%fused_computation.91 | convolution fusion | flops 9720299520 | bytes 45613056 | tf_op jit(solution)/shard_map/dot_general | solution.py:143
  294.8 46.8 %all-to-all-done.2 = bf16[8,256,768]{2,1,0:T(8,128)(2,1)} async-done(((bf16[8,256,768]{2,1,0:T(8,128)(2,1)}), bf16[8,256,768]{2,1,0:T(8,128)(2,1)}, u32[]{:S(2)}, u32[]{:S(2)}) %all-to-all-start.2) | async-done | bytes 3145760 | tf_op jit(solution)/shard_map/all_to_all | solution.py:158
  341.6 15.4 %fusion.61 = bf16[1,3072,768]{2,1,0:T(8,128)(2,1)} fusion(bf16[2048,3072]{1,0:T(8,128)(2,1)} %get-tuple-element.449, bf16[2048,768]{1,0:T(8,128)(2,1)} %bitcast.19), kind=kOutput, calls=%fused_computation.107 | convolution fusion | flops 9666035712 | bytes 20447232 | tf_op jit(solution)/shard_map/dot_general | solution.py:44
  357.0 16.0 %fusion.74 = bf16[2048,768]{1,0:T(8,128)(2,1)} fusion(bf16[2048,3072]{1,0:T(8,128)(2,1)} %get-tuple-element.449, bf16[1,3072,768]{2,1,0:T(8,128)(2,1)} %all-gather.11.cloned.1.call-done), kind=kOutput, calls=%fused_computation.120 | convolution fusion | flops 9665249280 | bytes 20447232 | tf_op jit(solution)/shard_map/dot_general | solution.py:145
  373.0 3.7 all-to-all-start.1
  376.8 30.1 %fusion.52 = bf16[2048,3072]{1,0:T(8,128)(2,1)} fusion(f32[2048,3072]{1,0:T(8,128)} %get-tuple-element.450, bf16[2048,768]{1,0:T(8,128)(2,1)} %bitcast.19, bf16[1,3072,768]{2,1,0:T(8,128)(2,1)} %all-gather.11.cloned.1.call-done), kind=kOutput, calls=%fused_computation.90 | convolution fusion | flops 9783214080 | bytes 45613056 | tf_op jit(solution)/shard_map/dot_general | solution.py:50
  406.9 14.7 %fusion.60 = bf16[1,768,3072]{2,1,0:T(8,128)(2,1)} fusion(bf16[2048,768]{1,0:T(8,128)(2,1)S(1)} %bitcast.167, bf16[2048,3072]{1,0:T(8,128)(2,1)} %fusion.52), kind=kOutput, calls=%fused_computation.106 | convolution fusion | flops 9666035712 | bytes 20447232 | tf_op jit(solution)/shard_map/dot_general | solution.py:44
  421.6 15.9 %fusion.71 = bf16[2048,768]{1,0:T(8,128)(2,1)} fusion(bf16[2048,3072]{1,0:T(8,128)(2,1)} %fusion.52, bf16[1,768,3072]{2,1,0:T(8,128)(2,1)} %all-gather.9.cloned.1.call-done), kind=kOutput, calls=%fused_computation.119 | convolution fusion | flops 9665249280 | bytes 20447232 | tf_op jit(solution)/shard_map/dot_general | solution.py:50
  437.5 9.6 %all-to-all-done.1 = bf16[8,256,768]{2,1,0:T(8,128)(2,1)S(1)} async-done(((bf16[8,256,768]{2,1,0:T(8,128)(2,1)}), bf16[8,256,768]{2,1,0:T(8,128)(2,1)S(1)}, u32[]{:S(2)}, u32[]{:S(2)}) %all-to-all-start.1) | async-done | bytes 3145760 | tf_op jit(solution)/shard_map/all_to_all | solution.py:148
  447.1 4.5 all-to-all-start.3
  451.6 2.6 copy.55
  454.2 5.2 gather_fusion.1
  459.4 2.6 copy.54
  462.0 59.7 %all-to-all-done.3 = bf16[8,256,768]{2,1,0:T(8,128)(2,1)} async-done(((bf16[8,256,768]{2,1,0:T(8,128)(2,1)}), bf16[8,256,768]{2,1,0:T(8,128)(2,1)}, u32[]{:S(2)}, u32[]{:S(2)}) %all-to-all-start.3) | async-done | bytes 3145760 | tf_op jit(solution)/shard_map/all_to_all | solution.py:180
  521.7 7.9 gather_fusion.2
  529.6 2.7 copy.56
  532.4 3.5 fusion.89
  535.9 2.9 fusion.87
  546.3 4.4 fusion.96
  550.8 172.4 %while.34 = (s32[]{:T(128)}, f32[1024,12,64]{0,2,1:T(8,128)}, f32[1024,12,64]{0,2,1:T(8,128)}, bf16[2,512,12,64]{1,3,2,0:T(8,128)(2,1)}, bf16[2,512,12,64]{1,3,2...) while((s32[]{:T(128)}, f32[1024,12,64]{0,2,1:T(8,128)}, ...), condition=%wide.region_17.18_spmd.clone, body=%wide.region_15.17_spmd.clone.sunk | while | flops 4126812160 | bytes 225640688 | solution.py:228
  552.9 11.7 %fusion.163 = f32[12,512,1024]{2,1,0:T(8,128)} fusion(bf16[1024,12,64]{0,2,1:T(8,128)(2,1)S(1)} %get-tuple-element.628, bf16[2,512,12,64]{1,3,2,0:T(8,128)(2,1)} %get-tuple-element.626, s32[]{:T(128)S(6)} %copy.88), kind=kOutput, calls=%fused_computation.53.clone.1 | convolution fusion | flops 805306368 | bytes 27525124 | tf_op jit(solution)/shard_map/while/body/eval_jaxpr/qhd,khd->hqk/dot_general | solution.py:67
  564.6 13.7 %bitcast_add_fusion.5 = f32[1024,12,64]{0,2,1:T(8,128)} fusion(f32[1024,12,64]{0,2,1:T(8,128)} %get-tuple-element.612, f32[12,512,1024]{2,1,0:T(8,128)} %fusion.163, f32[12,512]{1,0:T(8,128)S(1)} %dynamic-slice_bitcast_fusion.2, pred[512,1024]{1,0:T(8,128)(4,1)S(1)} %fusion.164, pred[]{:T(512)S(6)} %compare.43, ...), kind=kOutput, calls=%fused_computation.44.clone.1 | convolution fusion | flops 832045056 | bytes 32800772 | tf_op jit(solution)/shard_map/while/body/eval_jaxpr/hqk,qhd->khd/dot_general | solution.py:209
  578.4 18.3 %multiply_reduce_fusion.4 = (f32[12,512]{1,0:T(8,128)S(1)}, f32[12,512,1024]{2,1,0:T(8,128)}) fusion(f32[12,512,1024]{2,1,0:T(8,128)} %fusion.163, f32[12,512]{1,0:T(8,128)S(1)} %dynamic-slice_bitcast_fusion.2, pred[512,1024]{1,0:T(8,128)(4,1)S(1)} %fusion.164, bf16[1024,12,64]{0,2,1:T(8,128)(2,1)} %get-tuple-element.631, ...), kind=kOutput, calls=%fused_computation.39.clone.1 | convolution fusion | flops 836757504 | bytes 53264388 | tf_op jit(solution)/shard_map/while/body/eval_jaxpr/qhd,khd->hqk/dot_general | solution.py:206
  596.7 21.8 %multiply_convert_fusion.4 = bf16[12,512,1024]{2,1,0:T(8,128)(2,1)} fusion(f32[12,512,1024]{2,1,0:T(8,128)} %get-tuple-element.572, f32[12,512,1024]{2,1,0:T(8,128)} %fusion.163, f32[12,512]{1,0:T(8,128)S(1)} %get-tuple-element.573, f32[12,512]{1,0:T(8,128)S(1)} %dynamic-slice_bitcast_fusion.2, pred[512,1024]{1,0:T(8,128)(4,1)S(1)} %fusion.164), kind=kLoop, calls=%fused_computation.38.clone.1 | loop fusion | flops 37748736 | bytes 63488000 | tf_op jit(solution)/shard_map/while/body/eval_jaxpr/convert_element_type | solution.py:213
  618.5 9.5 %bitcast_dynamic-update-slice_fusion.5 = bf16[2,512,12,64]{1,3,2,0:T(8,128)(2,1)} fusion(bf16[2,512,12,64]{1,3,2,0:T(8,128)(2,1)} %get-tuple-element.613, s32[]{:T(128)S(6)} %copy.88, bf16[12,512,1024]{2,1,0:T(8,128)(2,1)} %multiply_convert_fusion.4, bf16[1024,12,64]{0,2,1:T(8,128)(2,1)S(1)} %get-tuple-element.628), kind=kOutput, calls=%fused_computation.48.clone.1 | convolution fusion | flops 805699584 | bytes 15728644 | tf_op jit(solution)/shard_map/while/body/eval_jaxpr/hqk,khd->qhd/dot_general | solution.py:215
  628.1 8.7 %bitcast_add_fusion.4 = f32[1024,12,64]{0,2,1:T(8,128)} fusion(f32[1024,12,64]{0,2,1:T(8,128)} %get-tuple-element.611, bf16[12,512,1024]{2,1,0:T(8,128)(2,1)} %multiply_convert_fusion.4, pred[]{:T(512)S(6)} %compare.43, bf16[2,512,12,64]{1,3,2,0:T(8,128)(2,1)S(1)} %copy-done.7, s32[]{:T(128)S(6)} %copy.88), kind=kOutput, calls=%fused_computation.45.clone.1 | convolution fusion | flops 807665664 | bytes 19660804 | tf_op jit(solution)/shard_map/while/body/eval_jaxpr/hqk,qhd->khd/dot_general | solution.py:220
  638.6 11.5 %fusion.163 = f32[12,512,1024]{2,1,0:T(8,128)} fusion(bf16[1024,12,64]{0,2,1:T(8,128)(2,1)S(1)} %get-tuple-element.628, bf16[2,512,12,64]{1,3,2,0:T(8,128)(2,1)} %get-tuple-element.626, s32[]{:T(128)S(6)} %copy.88), kind=kOutput, calls=%fused_computation.53.clone.1 | convolution fusion | flops 805306368 | bytes 27525124 | tf_op jit(solution)/shard_map/while/body/eval_jaxpr/qhd,khd->hqk/dot_general | solution.py:67
  650.2 14.3 %bitcast_add_fusion.5 = f32[1024,12,64]{0,2,1:T(8,128)} fusion(f32[1024,12,64]{0,2,1:T(8,128)} %get-tuple-element.612, f32[12,512,1024]{2,1,0:T(8,128)} %fusion.163, f32[12,512]{1,0:T(8,128)S(1)} %dynamic-slice_bitcast_fusion.2, pred[512,1024]{1,0:T(8,128)(4,1)S(1)} %fusion.164, pred[]{:T(512)S(6)} %compare.43, ...), kind=kOutput, calls=%fused_computation.44.clone.1 | convolution fusion | flops 832045056 | bytes 32800772 | tf_op jit(solution)/shard_map/while/body/eval_jaxpr/hqk,qhd->khd/dot_general | solution.py:209
  664.5 18.1 %multiply_reduce_fusion.4 = (f32[12,512]{1,0:T(8,128)S(1)}, f32[12,512,1024]{2,1,0:T(8,128)}) fusion(f32[12,512,1024]{2,1,0:T(8,128)} %fusion.163, f32[12,512]{1,0:T(8,128)S(1)} %dynamic-slice_bitcast_fusion.2, pred[512,1024]{1,0:T(8,128)(4,1)S(1)} %fusion.164, bf16[1024,12,64]{0,2,1:T(8,128)(2,1)} %get-tuple-element.631, ...), kind=kOutput, calls=%fused_computation.39.clone.1 | convolution fusion | flops 836757504 | bytes 53264388 | tf_op jit(solution)/shard_map/while/body/eval_jaxpr/qhd,khd->hqk/dot_general | solution.py:206
  682.6 21.2 %multiply_convert_fusion.4 = bf16[12,512,1024]{2,1,0:T(8,128)(2,1)} fusion(f32[12,512,1024]{2,1,0:T(8,128)} %get-tuple-element.572, f32[12,512,1024]{2,1,0:T(8,128)} %fusion.163, f32[12,512]{1,0:T(8,128)S(1)} %get-tuple-element.573, f32[12,512]{1,0:T(8,128)S(1)} %dynamic-slice_bitcast_fusion.2, pred[512,1024]{1,0:T(8,128)(4,1)S(1)} %fusion.164), kind=kLoop, calls=%fused_computation.38.clone.1 | loop fusion | flops 37748736 | bytes 63488000 | tf_op jit(solution)/shard_map/while/body/eval_jaxpr/convert_element_type | solution.py:213
  703.9 9.6 %bitcast_dynamic-update-slice_fusion.5 = bf16[2,512,12,64]{1,3,2,0:T(8,128)(2,1)} fusion(bf16[2,512,12,64]{1,3,2,0:T(8,128)(2,1)} %get-tuple-element.613, s32[]{:T(128)S(6)} %copy.88, bf16[12,512,1024]{2,1,0:T(8,128)(2,1)} %multiply_convert_fusion.4, bf16[1024,12,64]{0,2,1:T(8,128)(2,1)S(1)} %get-tuple-element.628), kind=kOutput, calls=%fused_computation.48.clone.1 | convolution fusion | flops 805699584 | bytes 15728644 | tf_op jit(solution)/shard_map/while/body/eval_jaxpr/hqk,khd->qhd/dot_general | solution.py:215
  713.5 9.5 %bitcast_add_fusion.4 = f32[1024,12,64]{0,2,1:T(8,128)} fusion(f32[1024,12,64]{0,2,1:T(8,128)} %get-tuple-element.611, bf16[12,512,1024]{2,1,0:T(8,128)(2,1)} %multiply_convert_fusion.4, pred[]{:T(512)S(6)} %compare.43, bf16[2,512,12,64]{1,3,2,0:T(8,128)(2,1)S(1)} %copy-done.7, s32[]{:T(128)S(6)} %copy.88), kind=kOutput, calls=%fused_computation.45.clone.1 | convolution fusion | flops 807665664 | bytes 19660804 | tf_op jit(solution)/shard_map/while/body/eval_jaxpr/hqk,qhd->khd/dot_general | solution.py:220
  723.2 3.2 copy.60
  727.1 3.0 convert.14
  731.3 6.9 fusion.90
  741.1 9.5 %fusion.83 = (f32[768]{0:T(1024)S(1)}, f32[1024]{0:T(1024)S(1)}, f32[1024]{0:T(1024)S(1)}, f32[1024,768]{0,1:T(8,128)}) fusion(bf16[1024,768]{0,1:T(8,128)(2,1)S(1)} %copy-done.12, f32[1024]{0:T(1024)S(1)} %copy-done.39, f32[1024]{0:T(1024)S(1)} %copy-done.35, f32[768]{0:T(1024)S(1)} %copy-done.37, bf16[768,2304]{1,0:T(8,128)(2,1)} %all-gather.5.cloned.1.call-done, ...), kind=kOutput, calls=%fused_computation.127 | convolution fusion | flops 3645109504 | bytes 12998656 | tf_op jit(solution)/shard_map/dot_general | solution.py:50
  750.7 38.1 %all-reduce.4 = (f32[768]{0:T(1024)S(1)}, f32[768]{0:T(1024)S(1)}) all-reduce(f32[768]{0:T(1024)S(1)} %get-tuple-element.392, f32[768]{0:T(1024)S(1)} %copy-done.40), channel_id=4, replica_groups=mesh['dp'=4,'expert'=8] {'dp','expert'}, use_global_device_ids=true, to_apply=%region_23.24.clone | all-reduce | flops 1536 | bytes 12288
  789.9 3.9 fusion.82
  795.3 2.9 convert_element_type.143
  798.2 2.9 convert_element_type.140
  801.1 55.4 %reduce-scatter.5.cloned.1.call-done = f32[24,2304]{1,0:T(8,128)} async-done(((f32[768,2304]{1,0:T(8,128)}), f32[24,2304]{1,0:T(8,128)}) %reduce-scatter.5.cloned.1.call-update) | async-done | bytes 221200 | tf_op jit(solution)/shard_map/reduce_scatter | solution.py:247
  (189 shorter events, 47.7 us)
Async XLA Ops:
  7.2 47.3 %copy-start = (s32[50304]{0:T(1024)S(1)}, s32[50304]{0:T(1024)}, u32[]{:S(2)}) copy-start(s32[50304]{0:T(1024)} %param.16) | copy-start | bytes 603652
  7.2 56.9 %copy-start.22 = (bf16[1024,768]{1,0:T(8,128)(2,1)S(1)}, bf16[1024,768]{1,0:T(8,128)(2,1)}, u32[]{:S(2)}) copy-start(bf16[1024,768]{1,0:T(8,128)(2,1)} %param.14) | copy-start | bytes 4718596
  7.2 66.8 %all-gather.5.cloned.1.call-start = ((), (), s32[]{:S(2)}) async-start(), calls=%async_computation.8 | async-start | bytes 3649536 | tf_op jit(solution)/shard_map/all_gather | solution.py:57
  7.9 167.7 %all-gather.7.cloned.1.call-start = ((), (), s32[]{:S(2)}) async-start(), calls=%async_computation.9 | async-start | bytes 1216512 | tf_op jit(solution)/shard_map/all_gather | solution.py:58
  8.7 263.6 %all-gather.9.cloned.1.call-start = ((), (), s32[]{:S(2)}) async-start(), calls=%async_computation.10 | async-start | bytes 5898240 | tf_op jit(solution)/shard_map/all_gather | solution.py:138
  53.2 20.8 %copy-start.36 = (f32[768]{0:T(1024)}, f32[768]{0:T(1024)S(1)}, u32[]{:S(2)}) copy-start(f32[768]{0:T(1024)S(1)} %convert_element_type.120) | copy-start | bytes 9220
  64.9 15.5 %copy-start.11 = (bf16[1024,768]{0,1:T(8,128)(2,1)}, bf16[1024,768]{0,1:T(8,128)(2,1)S(1)}, u32[]{:S(2)}) copy-start(bf16[1024,768]{0,1:T(8,128)(2,1)S(1)} %copy.47) | copy-start | bytes 4718596
  65.2 15.3 %copy-start.34 = (f32[1024]{0:T(1024)}, f32[1024]{0:T(1024)S(1)}, u32[]{:S(2)}) copy-start(f32[1024]{0:T(1024)S(1)} %broadcast_multiply_fusion.5) | copy-start | bytes 12292
  65.6 14.8 %copy-start.38 = (f32[1024]{0:T(1024)}, f32[1024]{0:T(1024)S(1)}, u32[]{:S(2)}) copy-start(f32[1024]{0:T(1024)S(1)} %add_rsqrt_fusion.1) | copy-start | bytes 12292
  95.9 23.2 %copy-start.8 = (bf16[1024,12,64]{0,2,1:T(8,128)(2,1)S(1)}, bf16[1024,12,64]{0,2,1:T(8,128)(2,1)}, u32[]{:S(2)}) copy-start(bf16[1024,12,64]{0,2,1:T(8,128)(2,1)} %get-tuple-element.596) | copy-start | bytes 4718596 | tf_op jit(solution)/shard_map/while
  106.7 15.6 %copy-start.2 = (f32[12,512,1024]{2,1,0:T(8,128)S(1)}, f32[12,512,1024]{2,1,0:T(8,128)}, u32[]{:S(2)}) copy-start(f32[12,512,1024]{2,1,0:T(8,128)} %get-tuple-element.558) | copy-start | bytes 75497472 | tf_op jit(solution)/shard_map/while
  136.5 23.6 %copy-start.8 = (bf16[1024,12,64]{0,2,1:T(8,128)(2,1)S(1)}, bf16[1024,12,64]{0,2,1:T(8,128)(2,1)}, u32[]{:S(2)}) copy-start(bf16[1024,12,64]{0,2,1:T(8,128)(2,1)} %get-tuple-element.596) | copy-start | bytes 4718596 | tf_op jit(solution)/shard_map/while
  147.6 15.6 %copy-start.2 = (f32[12,512,1024]{2,1,0:T(8,128)S(1)}, f32[12,512,1024]{2,1,0:T(8,128)}, u32[]{:S(2)}) copy-start(f32[12,512,1024]{2,1,0:T(8,128)} %get-tuple-element.558) | copy-start | bytes 75497472 | tf_op jit(solution)/shard_map/while
  175.6 5.0 copy-start.3
  175.6 5.0 copy-start.6
  175.6 5.0 copy-start.26
  175.6 5.0 copy-start.43
  180.6 1.6 copy-start.9
  180.6 1.6 copy-start.30
  180.6 2.0 copy-start.28
  182.3 1.1 copy-start.32
  191.0 75.8 %all-to-all-start = ((bf16[8,256,768]{2,1,0:T(8,128)(2,1)}), bf16[8,256,768]{2,1,0:T(8,128)(2,1)S(1)}, u32[]{:S(2)}, u32[]{:S(2)}) async-start(bf16[8,256,768]{2,1,0:T(8,128)(2,1)} %bitcast.12), calls=%async_computation | async-start | bytes 6291456 | tf_op jit(solution)/shard_map/all_to_all | solution.py:130
  266.8 5.5 copy-start.20
  266.8 74.8 %all-to-all-start.2 = ((bf16[8,256,768]{2,1,0:T(8,128)(2,1)}), bf16[8,256,768]{2,1,0:T(8,128)(2,1)}, u32[]{:S(2)}, u32[]{:S(2)}) async-start(bf16[8,256,768]{2,1,0:T(8,128)(2,1)} %bitcast.18), calls=%async_computation.2 | async-start | bytes 6291456 | tf_op jit(solution)/shard_map/all_to_all | solution.py:158
  271.3 85.8 %all-gather.11.cloned.1.call-start = ((), (), s32[]{:S(2)}) async-start(), calls=%async_computation.11 | async-start | bytes 5898240 | tf_op jit(solution)/shard_map/all_gather | solution.py:139
  271.8 523.5 %reduce-scatter.11.cloned.1.call-start = ((), (), s32[]{:S(2)}) async-start(), calls=%async_computation.15 | async-start | bytes 5898240 | tf_op jit(solution)/shard_map/reduce_scatter | solution.py:176
  373.0 74.0 %all-to-all-start.1 = ((bf16[8,256,768]{2,1,0:T(8,128)(2,1)}), bf16[8,256,768]{2,1,0:T(8,128)(2,1)S(1)}, u32[]{:S(2)}, u32[]{:S(2)}) async-start(bf16[8,256,768]{2,1,0:T(8,128)(2,1)} %bitcast.168), calls=%async_computation.1 | async-start | bytes 6291456 | tf_op jit(solution)/shard_map/all_to_all | solution.py:148
  376.8 421.4 %reduce-scatter.9.cloned.1.call-start = ((), (), s32[]{:S(2)}) async-start(), calls=%async_computation.14 | async-start | bytes 5898240 | tf_op jit(solution)/shard_map/reduce_scatter | solution.py:173
  376.8 30.1 %copy-start.21 = (bf16[8,256,768]{2,1,0:T(8,128)(2,1)S(1)}, bf16[8,256,768]{2,1,0:T(8,128)(2,1)}, u32[]{:S(2)}) copy-start(bf16[8,256,768]{2,1,0:T(8,128)(2,1)} %copy-done.20) | copy-start | bytes 9437188
  447.1 74.6 %all-to-all-start.3 = ((bf16[8,256,768]{2,1,0:T(8,128)(2,1)}), bf16[8,256,768]{2,1,0:T(8,128)(2,1)}, u32[]{:S(2)}, u32[]{:S(2)}) async-start(bf16[8,256,768]{2,1,0:T(8,128)(2,1)} %bitcast.169), calls=%async_computation.3 | async-start | bytes 6291456 | tf_op jit(solution)/shard_map/all_to_all | solution.py:180
  451.5 2.7 copy-start.41
  451.6 349.5 %reduce-scatter.7.cloned.1.call-start = ((), (), s32[]{:S(2)}) async-start(), calls=%async_computation.13 | async-start | bytes 2433024 | tf_op jit(solution)/shard_map/reduce_scatter | solution.py:248
  521.7 10.6 %copy-start.29 = (f32[1024]{0:T(1024)S(1)}, f32[1024]{0:T(1024)}, u32[]{:S(2)}) copy-start(f32[1024]{0:T(1024)} %copy-done.28) | copy-start | bytes 12292
  521.7 10.6 %copy-start.31 = (f32[768]{0:T(1024)S(1)}, f32[768]{0:T(1024)}, u32[]{:S(2)}) copy-start(f32[768]{0:T(1024)} %convert_element_type.125) | copy-start | bytes 9220
  521.7 10.6 %copy-start.33 = (f32[1024]{0:T(1024)S(1)}, f32[1024]{0:T(1024)}, u32[]{:S(2)}) copy-start(f32[1024]{0:T(1024)} %copy-done.32) | copy-start | bytes 12292
  529.6 2.7 copy-start.10
  532.3 3.5 copy-start.14
  532.4 3.5 copy-start.18
  532.4 3.5 copy-start.19
  535.9 4.6 copy-start.42
  538.8 1.6 copy-start.15
  543.9 2.5 copy-start.16
  546.3 4.5 copy-start.4
  546.3 4.5 copy-start.27
  546.3 4.5 copy-start.44
  550.7 305.7 %reduce-scatter.5.cloned.1.call-start = ((), (), s32[]{:S(2)}) async-start(), calls=%async_computation.12 | async-start | bytes 7299072 | tf_op jit(solution)/shard_map/reduce_scatter | solution.py:247
  552.9 11.7 %copy-start.13 = (bf16[2,512,12,64]{1,3,2,0:T(8,128)(2,1)S(1)}, bf16[2,512,12,64]{1,3,2,0:T(8,128)(2,1)}, u32[]{:S(2)}) copy-start(bf16[2,512,12,64]{1,3,2,0:T(8,128)(2,1)} %get-tuple-element.630) | copy-start | bytes 4718596 | tf_op jit(solution)/shard_map/while
  618.5 9.6 %copy-start.7 = (bf16[2,512,12,64]{1,3,2,0:T(8,128)(2,1)S(1)}, bf16[2,512,12,64]{1,3,2,0:T(8,128)(2,1)}, u32[]{:S(2)}) copy-start(bf16[2,512,12,64]{1,3,2,0:T(8,128)(2,1)} %get-tuple-element.626) | copy-start | bytes 4718596 | tf_op jit(solution)/shard_map/while
  638.6 11.5 %copy-start.13 = (bf16[2,512,12,64]{1,3,2,0:T(8,128)(2,1)S(1)}, bf16[2,512,12,64]{1,3,2,0:T(8,128)(2,1)}, u32[]{:S(2)}) copy-start(bf16[2,512,12,64]{1,3,2,0:T(8,128)(2,1)} %get-tuple-element.630) | copy-start | bytes 4718596 | tf_op jit(solution)/shard_map/while
  703.9 9.6 %copy-start.7 = (bf16[2,512,12,64]{1,3,2,0:T(8,128)(2,1)S(1)}, bf16[2,512,12,64]{1,3,2,0:T(8,128)(2,1)}, u32[]{:S(2)}) copy-start(bf16[2,512,12,64]{1,3,2,0:T(8,128)(2,1)} %get-tuple-element.626) | copy-start | bytes 4718596 | tf_op jit(solution)/shard_map/while
  723.2 3.6 copy-start.5
  726.8 3.3 copy-start.23
  727.1 3.1 copy-start.24
  727.1 4.2 copy-start.12
  727.1 4.2 copy-start.35
  727.1 4.2 copy-start.37
  727.1 4.2 copy-start.39
  730.1 1.1 copy-start.25
  738.1 1.4 copy-start.17
  741.1 9.5 %copy-start.40 = (f32[768]{0:T(1024)S(1)}, f32[768]{0:T(1024)}, u32[]{:S(2)}) copy-start(f32[768]{0:T(1024)} %get-tuple-element.390) | copy-start | bytes 9220
  793.8 62.7 %copy-start.1 = (s32[50304]{0:T(1024)S(1)}, s32[50304]{0:T(1024)}, u32[]{:S(2)}) copy-start(s32[50304]{0:T(1024)} %param.16) | copy-start | bytes 603652
Sparse Core Ops, SparseCore 0:
  11.0 62.9 all-gather.4
  77.0 52.9 all-gather.6
  131.6 36.3 all-gather.8
  273.4 38.1 all-gather.10
  357.1 46.2 reduce-scatter.10
  421.7 48.1 reduce-scatter.8
  550.9 97.4 reduce-scatter.6
  738.3 118.0 reduce-scatter.4
where the time goes:
time: 870 us; the launch traced here: 863 us
  matrix products  311 us (36%)
  waiting for transfers between devices  246 us (28%)
  other arithmetic  98.1 us (11%)
  local copies, waits for them, and re-layouts  94.6 us (11%)
  blocking collectives  80.1 us (9%)
  starting transfers between devices  18 us (2%)
  between operations  15 us (2%)
    unnamed x2, blocking collectives  80.1 us
    all_to_all x1, waiting for transfers between devices, per_device(): lax.all_to_all(send_rows.reshape(n_expert, slot_most, model_width), 'expe...  63.3 us
    all_to_all x1, waiting for transfers between devices, per_device(): lax.all_to_all(grad_act.reshape(n_expert, slot_most, model_width), 'exper...  59.7 us
    dot_general x4, matrix products, contract_cols(): lax.dot_general(left, right, (((1,), (1,)), ((), ())), preferred_element_...  57 us
    reduce_scatter x1, waiting for transfers between devices, per_device(): lax.psum_scatter(grad_qkv_proj, ('dp', 'expert'), scatter_dimension=0, ti...  55.4 us
    all_to_all x1, waiting for transfers between devices, per_device(): lax.all_to_all(grad_send.reshape(n_expert, slot_most, model_width), 'expe...  46.8 us
    dot_general x4, matrix products, block_scores(): jnp.einsum('qhd,khd->hqk', query_block, key_rows, preferred_element_type=...  45.1 us
    convert_element_type x2, other arithmetic, backward_block(): grad_scores = grad_scores.astype(jnp.bfloat16)  43.1 us
  transfers between devices with their start and end apart: 12, of which 6 were waited for; matrix products, arithmetic and copies ran while one was open for 57% of the time, Pallas kernels for 0%

commit v1 on v0

v1 whole, which is shorter than its diff:
```python
import jax
import jax.numpy as jnp
from jax import lax
from jax.experimental import pallas as pl
from jax.experimental.pallas import tpu as pltpu
from jax.sharding import PartitionSpec as P

HEADS = 12
SEQ = 1024


EPS = 1e-05
NEG = -1e30
GELU_C = 0.7978845608028654


def gelu_tanh(values):
    return 0.5 * values * (1.0 + jnp.tanh(GELU_C * (values + 0.044715 * values * values * values)))


def gelu_slope(values):
    inner = jnp.tanh(GELU_C * (values + 0.044715 * values * values * values))
    return 0.5 * (1.0 + inner) + 0.5 * values * (1.0 - inner * inner) * GELU_C * (
        1.0 + 3.0 * 0.044715 * values * values
    )


def norm_parts(values):
    centre = jnp.mean(values, axis=-1, keepdims=True)
    shifted = values - centre
    spread = jnp.mean(shifted * shifted, axis=-1, keepdims=True)
    inverse = lax.rsqrt(spread + EPS)
    return (shifted * inverse, inverse)


def norm_grad(upstream, gain, normed, inverse):
    scaled = upstream * gain
    return inverse * (
        scaled
        - jnp.mean(scaled, axis=-1, keepdims=True)
        - normed * jnp.mean(scaled * normed, axis=-1, keepdims=True)
    )


def contract_rows(left, right):
    return lax.dot_general(
        left, right, (((0,), (0,)), ((), ())), preferred_element_type=jnp.float32
    )


def contract_cols(left, right):
    return lax.dot_general(
        left, right, (((1,), (1,)), ((), ())), preferred_element_type=jnp.float32
    )


F32 = jnp.float32
BF = jnp.bfloat16
QB = 256
def dot(a,b): return jnp.dot(a,b,preferred_element_type=F32)
def dot_nt(a,b): return lax.dot_general(a,b,(((1,),(1,)),((),())),preferred_element_type=F32)

def head_masks():
    lane = lax.broadcasted_iota(jnp.int32,(1,128),1)
    lo = jnp.where(lane<64,1.0,0.0)
    return [lo.astype(BF),(1.0-lo).astype(BF)]

def attn_fwd_pair(p, seq, width, qkv_ref, ctx_ref, lse_ref):
    off = pl.multiple_of(p*128,128)
    masks = head_masks()
    lane_lo = lax.broadcasted_iota(jnp.int32,(QB,128),1)<64
    nb = seq//QB
    kp = qkv_ref[:, pl.ds(pl.multiple_of(width+off,128),128)]
    vp = qkv_ref[:, pl.ds(pl.multiple_of(2*width+off,128),128)]
    vts = [(vp*m+(1-m)).T for m in masks]
    causal = lax.broadcasted_iota(jnp.int32,(QB,QB),0)<=lax.broadcasted_iota(jnp.int32,(QB,QB),1)
    for i in range(nb):
        nk=(i+1)*QB
        qb = qkv_ref[pl.ds(i*QB,QB), pl.ds(off,128)]
        outs=[]
        for hh in range(2):
            qh = qb*(masks[hh]*0.125).astype(BF)
            st = dot_nt(kp[:nk], qh)
            diag = jnp.where(causal, st[nk-QB:], -1e30)
            m = jnp.max(diag,axis=0,keepdims=True)
            if i:
                m = jnp.maximum(m, jnp.max(st[:nk-QB],axis=0,keepdims=True))
            pd = jnp.exp(diag-m).astype(BF)
            ot = dot(vts[hh][:, nk-QB:nk], pd)
            if i:
                po = jnp.exp(st[:nk-QB]-m).astype(BF)
                ot = ot + dot(vts[hh][:, :nk-QB], po)
            l = ot[64:65] if hh==0 else ot[0:1]
            outs.append((ot*(1.0/l)))
            lse_ref[pl.ds(2*p+hh,1), pl.ds(i*QB,QB)] = m+jnp.log(l)
        sub_lo = lax.broadcasted_iota(jnp.int32,(128,QB),0)<64
        o = jnp.where(sub_lo, outs[0], outs[1]).T
        ctx_ref[pl.ds(i*QB,QB), pl.ds(off,128)] = o.astype(BF)

def attn_bwd_pair(p, seq, width, qkv_ref, ctx_ref, lse_ref, do_ref, dqkv_ref, dqt_ref):
    off = pl.multiple_of(p*128,128)
    masks = head_masks()
    nb = seq//QB
    koff = pl.multiple_of(width+off,128); voff=pl.multiple_of(2*width+off,128)
    qp = qkv_ref[:, pl.ds(off,128)]
    kp = qkv_ref[:, pl.ds(koff,128)]
    dop = do_ref[:, pl.ds(off,128)]
    prod = dop.astype(F32)*ctx_ref[:, pl.ds(off,128)].astype(F32)
    sel = (lax.broadcasted_iota(jnp.int32,(8,128),1)//64 == lax.broadcasted_iota(jnp.int32,(8,128),0)).astype(F32)
    delta = lax.dot_general(sel, prod, (((1,),(1,)),((),())), preferred_element_type=F32, precision=lax.Precision.HIGHEST)
    causal = lax.broadcasted_iota(jnp.int32,(QB,QB),0)<=lax.broadcasted_iota(jnp.int32,(QB,QB),1)
    qs = [qp*(m*0.125).astype(BF) for m in masks]
    dos = [dop*m for m in masks]
    kts = [(kp*(m*0.125).astype(BF)).T for m in masks]
    lses = [lse_ref[pl.ds(2*p+hh,1), :] for hh in range(2)]
    for j in range(nb):
        q0=j*QB
        kj = qkv_ref[pl.ds(q0,QB), pl.ds(koff,128)]
        vj = qkv_ref[pl.ds(q0,QB), pl.ds(voff,128)]
        dk=None; dv=None; dq=None
        for hh in range(2):
            st = dot_nt(kj, qs[hh][q0:])
            pt = jnp.exp(st-lses[hh][:, q0:])
            dpt = dot_nt(vj, dos[hh][q0:])
            if nb-j>1:
                pt = jnp.concatenate([jnp.where(causal, pt[:, :QB], 0.0), pt[:, QB:]],axis=1)
            else:
                pt = jnp.where(causal, pt, 0.0)
            dst = (pt*(dpt-delta[hh:hh+1, q0:])).astype(BF)
            ptl = pt.astype(BF)
            a = dot(ptl, dos[hh][q0:]); b = dot(dst, qs[hh][q0:]); c = dot(kts[hh][:, q0:q0+QB], dst)
            dv = a if dv is None else dv+a
            dk = b if dk is None else dk+b
            dq = c if dq is None else dq+c
        dqkv_ref[pl.ds(q0,QB), pl.ds(koff,128)] = dk.astype(BF)
        dqkv_ref[pl.ds(q0,QB), pl.ds(voff,128)] = dv.astype(BF)
        if j==0:
            dqt_ref[...] = dq
        else:
            dqt_ref[:, pl.ds(q0,seq-q0)] += dq
    dqkv_ref[:, pl.ds(off,128)] = dqt_ref[...].T.astype(BF)

def fwd_kernel(act_ref, w_ref, qkv_ref, ctx_ref, lse_ref):
    seq,width = act_ref.shape
    @pl.loop(0, 3*width//256)
    def _(n):
        c = pl.ds(pl.multiple_of(n*256,256),256)
        qkv_ref[:, c] = dot(act_ref[...], w_ref[:, c]).astype(BF)
    @pl.loop(0, width//128)
    def _(p):
        attn_fwd_pair(p, seq, width, qkv_ref, ctx_ref, lse_ref)

def bwd_kernel(qkv_ref, ctx_ref, lse_ref, do_ref, dqkv_ref, dqt_ref):
    seq,width = ctx_ref.shape
    @pl.loop(0, width//128)
    def _(p):
        attn_bwd_pair(p, seq, width, qkv_ref, ctx_ref, lse_ref, do_ref, dqkv_ref, dqt_ref)


VM = pl.BlockSpec(memory_space=pltpu.VMEM)


def attention_forward(act, w):
    seq, width = act.shape
    return pl.pallas_call(
        fwd_kernel,
        out_shape=(
            jax.ShapeDtypeStruct((seq, 3 * width), BF),
            jax.ShapeDtypeStruct((seq, width), BF),
            jax.ShapeDtypeStruct((16, seq), F32),
        ),
        in_specs=[VM] * 2,
        out_specs=(VM,) * 3,
        compiler_params=pltpu.CompilerParams(vmem_limit_bytes=56 << 20),
    )(act, w)


def attention_backward(qkv, ctx, lse, do):
    seq, width = ctx.shape
    return pl.pallas_call(
        bwd_kernel,
        out_shape=jax.ShapeDtypeStruct((seq, 3 * width), BF),
        in_specs=[VM] * 4,
        out_specs=VM,
        scratch_shapes=[pltpu.VMEM((128, seq), F32)],
        compiler_params=pltpu.CompilerParams(vmem_limit_bytes=56 << 20),
    )(qkv, ctx, lse, do)


def attention_weights(gain_attn, gain_ffn, w_qkv, w_o):
    axes = ("dp", "expert")
    width = w_o.shape[1]
    packed = jnp.concatenate([w_o, gain_attn[:, None], gain_ffn[:, None]], axis=1)
    qkv_full = lax.all_gather(w_qkv, axes, axis=0, tiled=True)
    rest = lax.all_gather(packed, axes, axis=0, tiled=True)
    return qkv_full, rest[:, :width], rest[:, width], rest[:, width + 1]


def per_device(
    tokens_in, token_ids, hash_table, gain_attn, gain_ffn, w_qkv, w_o, w_in, w_out, cotangent
):
    tok_rows, model_width = tokens_in.shape
    n_expert = lax.axis_size("expert")
    slot_most = 2 * tok_rows // n_expert
    slot_count = n_expert * slot_most
    qkv_full, out_full, gain_one, gain_two = attention_weights(gain_attn, gain_ffn, w_qkv, w_o)
    gain_one = gain_one.astype(jnp.float32)
    gain_two = gain_two.astype(jnp.float32)
    inputs = tokens_in.astype(jnp.float32)
    normed_one, inverse_one = norm_parts(inputs)
    act_one = (normed_one * gain_one).astype(jnp.bfloat16)
    qkv, context, lse = attention_forward(act_one, qkv_full)
    mixed = inputs + jnp.dot(context, out_full, preferred_element_type=jnp.float32)
    normed_two, inverse_two = norm_parts(mixed)
    act_two = (normed_two * gain_two).astype(jnp.bfloat16)
    expert_ids = hash_table[token_ids]
    one_hot = (expert_ids[:, None] == jnp.arange(n_expert, dtype=jnp.int32)[None, :]).astype(
        jnp.int32
    )
    before = jnp.cumsum(one_hot, axis=0) - one_hot
    slot_index = expert_ids * slot_most + jnp.sum(before * one_hot, axis=1)
    send_rows = jnp.zeros((slot_count, model_width), jnp.bfloat16).at[slot_index].set(act_two)
    recv_rows = lax.all_to_all(
        send_rows.reshape(n_expert, slot_most, model_width),
        "expert",
        split_axis=0,
        concat_axis=0,
        tiled=True,
    ).reshape(slot_count, model_width)
    w_in_full, w_out_full = (
        lax.all_gather(w_in, "dp", axis=2, tiled=True),
        lax.all_gather(w_out, "dp", axis=1, tiled=True),
    )
    w_in_full = w_in_full[0]
    w_out_full = w_out_full[0]
    pre_act = jnp.dot(recv_rows, w_in_full, preferred_element_type=jnp.float32)
    hidden = gelu_tanh(pre_act).astype(jnp.bfloat16)
    expert_out = jnp.dot(hidden, w_out_full, preferred_element_type=jnp.float32).astype(
        jnp.bfloat16
    )
    returned = lax.all_to_all(
        expert_out.reshape(n_expert, slot_most, model_width),
        "expert",
        split_axis=0,
        concat_axis=0,
        tiled=True,
    ).reshape(slot_count, model_width)
    branch_out = returned[slot_index]
    block_out = (mixed + branch_out.astype(jnp.float32)).astype(jnp.bfloat16)
    grad_send = jnp.zeros((slot_count, model_width), jnp.bfloat16).at[slot_index].set(cotangent)
    grad_rows = lax.all_to_all(
        grad_send.reshape(n_expert, slot_most, model_width),
        "expert",
        split_axis=0,
        concat_axis=0,
        tiled=True,
    ).reshape(slot_count, model_width)
    grad_out_full = contract_rows(hidden, grad_rows)
    grad_hidden = contract_cols(grad_rows, w_out_full)
    grad_pre = (grad_hidden * gelu_slope(pre_act)).astype(jnp.bfloat16)
    grad_in_full = contract_rows(recv_rows, grad_pre)
    grad_act = contract_cols(grad_pre, w_in_full).astype(jnp.bfloat16)
    grad_w_in, grad_w_out = (
        lax.psum_scatter(
            grad_in_full[None].astype(jnp.bfloat16), "dp", scatter_dimension=2, tiled=True
        ).astype(jnp.float32),
        lax.psum_scatter(
            grad_out_full[None].astype(jnp.bfloat16), "dp", scatter_dimension=1, tiled=True
        ).astype(jnp.float32),
    )
    grad_back = lax.all_to_all(
        grad_act.reshape(n_expert, slot_most, model_width),
        "expert",
        split_axis=0,
        concat_axis=0,
        tiled=True,
    ).reshape(slot_count, model_width)
    grad_act_two = grad_back[slot_index].astype(jnp.float32)
    grad_gain_two = jnp.sum(grad_act_two * normed_two, axis=0)
    grad_mixed = cotangent.astype(jnp.float32) + norm_grad(
        grad_act_two, gain_two, normed_two, inverse_two
    )
    grad_branch = grad_mixed.astype(jnp.bfloat16)
    grad_out_proj = contract_rows(context, grad_branch)
    grad_context = contract_cols(grad_branch, out_full).astype(jnp.bfloat16)
    grad_qkv = attention_backward(qkv, context, lse, grad_context)
    grad_qkv_proj = contract_rows(act_one, grad_qkv)
    grad_act_one = contract_cols(grad_qkv, qkv_full)
    grad_gain_one = jnp.sum(grad_act_one * normed_one, axis=0)
    grad_tokens = (grad_mixed + norm_grad(grad_act_one, gain_one, normed_one, inverse_one)).astype(
        jnp.bfloat16
    )
    axes = ("dp", "expert")
    grad_w_qkv = lax.psum_scatter(
        grad_qkv_proj.astype(BF), axes, scatter_dimension=0, tiled=True
    ).astype(F32)
    grad_w_o = lax.psum_scatter(
        grad_out_proj.astype(BF), axes, scatter_dimension=0, tiled=True
    ).astype(F32)
    gains = lax.psum(jnp.stack([grad_gain_one, grad_gain_two]), axes)
    me = lax.axis_index("dp") * n_expert + lax.axis_index("expert")
    rows = gain_attn.shape[0]
    mine = lax.dynamic_slice(gains, (0, me * rows), (2, rows))
    grad_gain_attn, grad_gain_ffn = mine[0], mine[1]
    return (
        block_out,
        grad_tokens,
        grad_w_qkv,
        grad_w_o,
        grad_gain_attn,
        grad_gain_ffn,
        grad_w_in,
        grad_w_out,
    )


def solution(mesh):
    return jax.shard_map(
        per_device,
        mesh=mesh,
        in_specs=(
            P(("dp", "expert"), None),
            P(("dp", "expert")),
            P(),
            P(("dp", "expert")),
            P(("dp", "expert")),
            P(("dp", "expert"), None),
            P(("dp", "expert"), None),
            P("expert", None, "dp"),
            P("expert", "dp", None),
            P(("dp", "expert"), None),
        ),
        out_specs=(
            P(("dp", "expert"), None),
            P(("dp", "expert"), None),
            P(("dp", "expert"), None),
            P(("dp", "expert"), None),
            P(("dp", "expert")),
            P(("dp", "expert")),
            P("expert", None, "dp"),
            P("expert", "dp", None),
        ),
        check_vma=False,
    )
```

time: 870 us -> 858 us (0.986)
  waiting for transfers between devices: 246 us -> 505 us
  matrix products: 311 us -> 138 us
  Pallas kernels: 0 us -> 62.9 us
  other arithmetic: 98.1 us -> 37.7 us
  local copies, waits for them, and re-layouts: 94.6 us -> 34.8 us
  blocking collectives: 80.1 us -> 37.9 us
    dot_general x15 -> x0, matrix products: 169 us -> none  [the longest x4 45.1 us: block_scores(): jnp.einsum('qhd,khd->hqk', query_block, key_rows, preferred_element_type=...]
    all_gather x2, waiting for transfers between devices: 8.42 us -> 106 us  [the longest x1 59.2 us: attention_weights(): qkv_full = lax.all_gather(w_qkv, axes, axis=0, tiled=True)]
    unnamed x2 -> x0, blocking collectives: 80.1 us -> none
    pallas_call x0 -> x2, Pallas kernels: none -> 62.9 us  [the longest x1 33.1 us: attention_forward(): pl.pallas_call(fwd_kernel, out_shape=(jax.ShapeDtypeStruct((seq, 3 * widt...]
    all_to_all x1, waiting for transfers between devices: 9.6 us -> 60.9 us  [per_device(): lax.all_to_all(expert_out.reshape(n_expert, slot_most, model_width), 'exp...]
    reduce_scatter x2, waiting for transfers between devices: 55.4 us -> 106 us  [the longest x1 106 us: per_device(): lax.psum_scatter(grad_qkv_proj.astype(BF), axes, scatter_dimension=0, til...]
    reduce_scatter x1, waiting for transfers between devices: 0.01 us -> 47.7 us  [per_device(): lax.psum_scatter(grad_out_full[None].astype(jnp.bfloat16), 'dp', scatter_...]
    convert_element_type x4 -> x3, other arithmetic: 43.5 us -> 4.72 us  [the longest x1 1.67 us: per_device(): act_one = (normed_one * gain_one).astype(jnp.bfloat16)]
  transfers between devices with their start and end apart: 12 -> 12, of which waited for: 6 -> 9; matrix products, arithmetic and copies ran while one was open for 57% -> 17% of each run, Pallas kernels for 0% -> 7%
where the time goes in v1:
time: 858 us; the launch traced here: 849 us
  waiting for transfers between devices  505 us (59%)
  matrix products  138 us (16%)
  Pallas kernels  62.9 us (7%)
  blocking collectives  37.9 us (4%)
  other arithmetic  37.7 us (4%)
  local copies, waits for them, and re-layouts  34.8 us (4%)
  starting transfers between devices  17.3 us (2%)
  between operations  14.9 us (2%)
    reduce_scatter x1, waiting for transfers between devices, per_device(): lax.psum_scatter(grad_qkv_proj.astype(BF), axes, scatter_dimension=0, til...  106 us
    all_to_all x1, waiting for transfers between devices, per_device(): lax.all_to_all(send_rows.reshape(n_expert, slot_most, model_width), 'expe...  62.7 us
    all_to_all x1, waiting for transfers between devices, per_device(): lax.all_to_all(expert_out.reshape(n_expert, slot_most, model_width), 'exp...  60.9 us
    all_gather x1, waiting for transfers between devices, attention_weights(): qkv_full = lax.all_gather(w_qkv, axes, axis=0, tiled=True)  59.2 us
    dot_general x4, matrix products, contract_cols(): lax.dot_general(left, right, (((1,), (1,)), ((), ())), preferred_element_...  57.7 us
    all_to_all x1, waiting for transfers between devices, per_device(): lax.all_to_all(grad_act.reshape(n_expert, slot_most, model_width), 'exper...  55.5 us
    all_to_all x1, waiting for transfers between devices, per_device(): lax.all_to_all(grad_send.reshape(n_expert, slot_most, model_width), 'expe...  48.4 us
    reduce_scatter x1, waiting for transfers between devices, per_device(): lax.psum_scatter(grad_out_full[None].astype(jnp.bfloat16), 'dp', scatter_...  47.7 us
  transfers between devices with their start and end apart: 12, of which 9 were waited for; matrix products, arithmetic and copies ran while one was open for 17% of the time, Pallas kernels for 7%

profile of v1, /device:TPU:0, one launch (start us, length us, event | category | flops | bytes accessed | tf_op | source)
XLA Modules:
  0.0 848.8 jit_solution(15215369278641986492)
XLA Ops:
  7.2 0.9 copy.23
  8.1 0.7 copy.24
  8.9 1.5 pad_maximum_fusion
  10.4 0.7 all-gather.7.cloned.1.call-update
  11.1 0.7 all-gather.9.cloned.1.call-update
  11.8 0.7 fusion.59
  12.5 6.1 gather_fusion
  18.7 2.3 reduce-window.6
  21.0 0.3 slice_reduce_fusion
  21.3 0.2 reduce-window.9
  21.4 0.1 add_bitcast_fusion
  21.5 0.3 convert_reduce_fusion
  21.8 0.6 fusion.38
  22.5 46.5 %all-gather.5.cloned.1.call-done = bf16[768,770]{1,0:T(8,128)(2,1)} async-done(((bf16[24,770]{1,0:T(8,128)(2,1)}), bf16[768,770]{1,0:T(8,128)(2,1)}) %all-gather.5.cloned.1.call-update) | async-done | bytes 1182736 | tf_op jit(solution)/shard_map/all_gather | solution.py:195
  69.0 1.3 convert_reduce_fusion.1
  70.3 1.7 fusion.31.act_ref
  72.0 59.2 %all-gather.7.cloned.1.call-done.w_ref = bf16[768,2304]{1,0:T(8,128)(2,1)} async-done(((bf16[24,2304]{1,0:T(8,128)(2,1)}), bf16[768,2304]{1,0:T(8,128)(2,1)}) %all-gather.7.cloned.1.call-update) | async-done | bytes 3538960 | tf_op jit(solution)/shard_map/all_gather | solution.py:194
  131.1 33.1 %shard_map.161 = (bf16[1024,2304]{1,0:T(8,128)(2,1)}, bf16[1024,768]{1,0:T(8,128)(2,1)}, f32[16,1024]{1,0:T(8,128)}) custom-call(bf16[1024,768]{1,0:T(8,128)(2,1)} %fusion.31.act_ref, bf16[768,2304]{1,0:T(8,128)(2,1)} %all-gather.7.cloned.1.call-done.w_ref), custom_call_target="tpu_custom_call" | custom-call | tf_op jit(solution)/shard_map/pallas_call | solution.py:165
  164.3 3.0 fusion.60
  167.3 0.5 multiply_reduce_fusion
  167.8 7.7 scatter_custom_fusion
  175.5 4.3 all-to-all-start
  179.7 0.2 all-gather.11.cloned.1.call-start
  180.0 0.3 all-gather.11.cloned.1.call-update
  180.3 7.9 scatter_custom_fusion.1
  188.2 62.7 %all-to-all-done = bf16[8,256,768]{2,1,0:T(8,128)(2,1)S(1)} async-done(((bf16[8,256,768]{2,1,0:T(8,128)(2,1)}), bf16[8,256,768]{2,1,0:T(8,128)(2,1)S(1)}, u32[]{:S(2)}, u32[]{:S(2)}) %all-to-all-start) | async-done | bytes 3145760 | tf_op jit(solution)/shard_map/all_to_all | solution.py:223
  250.9 4.5 all-to-all-start.2
  255.4 21.8 %multiply_convert_fusion = (bf16[2048,3072]{1,0:T(8,128)(2,1)}, f32[2048,3072]{1,0:T(8,128)}) fusion(bf16[2048,768]{1,0:T(8,128)(2,1)S(1)} %bitcast.72, bf16[1,768,3072]{2,1,0:T(8,128)(2,1)} %all-gather.9.cloned.1.call-done), kind=kOutput, calls=%fused_computation.14 | convolution fusion | flops 9720299520 | bytes 45613056 | tf_op jit(solution)/shard_map/dot_general | solution.py:236
  277.2 48.4 %all-to-all-done.2 = bf16[8,256,768]{2,1,0:T(8,128)(2,1)} async-done(((bf16[8,256,768]{2,1,0:T(8,128)(2,1)}), bf16[8,256,768]{2,1,0:T(8,128)(2,1)}, u32[]{:S(2)}, u32[]{:S(2)}) %all-to-all-start.2) | async-done | bytes 3145760 | tf_op jit(solution)/shard_map/all_to_all | solution.py:251
  325.7 30.1 %fusion.6 = bf16[2048,3072]{1,0:T(8,128)(2,1)} fusion(f32[2048,3072]{1,0:T(8,128)} %get-tuple-element.29, bf16[2048,768]{1,0:T(8,128)(2,1)} %bitcast.13, bf16[1,3072,768]{2,1,0:T(8,128)(2,1)} %all-gather.11.cloned.1.call-done), kind=kOutput, calls=%fused_computation.13 | convolution fusion | flops 9783214080 | bytes 45613056 | tf_op jit(solution)/shard_map/dot_general | solution.py:52
  355.7 14.5 %fusion.25 = bf16[2048,768]{1,0:T(8,128)(2,1)} fusion(bf16[2048,3072]{1,0:T(8,128)(2,1)} %fusion.6, bf16[1,768,3072]{2,1,0:T(8,128)(2,1)S(1)} %copy-done.20), kind=kOutput, calls=%fused_computation.41 | convolution fusion | flops 9665249280 | bytes 20447232 | tf_op jit(solution)/shard_map/dot_general | solution.py:52
  370.3 3.6 all-to-all-start.3
  373.9 15.4 %fusion.28 = bf16[2048,768]{1,0:T(8,128)(2,1)} fusion(bf16[2048,3072]{1,0:T(8,128)(2,1)} %get-tuple-element.28, bf16[1,3072,768]{2,1,0:T(8,128)(2,1)} %all-gather.11.cloned.1.call-done), kind=kOutput, calls=%fused_computation.42 | convolution fusion | flops 9665249280 | bytes 20447232 | tf_op jit(solution)/shard_map/dot_general | solution.py:238
  389.3 55.5 %all-to-all-done.3 = bf16[8,256,768]{2,1,0:T(8,128)(2,1)S(1)} async-done(((bf16[8,256,768]{2,1,0:T(8,128)(2,1)}), bf16[8,256,768]{2,1,0:T(8,128)(2,1)S(1)}, u32[]{:S(2)}, u32[]{:S(2)}) %all-to-all-start.3) | async-done | bytes 3145760 | tf_op jit(solution)/shard_map/all_to_all | solution.py:271
  444.8 4.4 all-to-all-start.1
  449.2 0.0 reduce-scatter.7.cloned.1.call-start
  449.3 5.4 gather_fusion.2
  454.7 3.8 fusion.43
  458.5 60.9 %all-to-all-done.1 = bf16[8,256,768]{2,1,0:T(8,128)(2,1)} async-done(((bf16[8,256,768]{2,1,0:T(8,128)(2,1)}), bf16[8,256,768]{2,1,0:T(8,128)(2,1)}, u32[]{:S(2)}, u32[]{:S(2)}) %all-to-all-start.1) | async-done | bytes 3145760 | tf_op jit(solution)/shard_map/all_to_all | solution.py:241
  519.4 8.0 gather_fusion.1
  527.4 4.1 fusion.41
  531.5 1.6 copy-done.7
  533.1 2.5 convolution_convert_fusion.4
  535.7 0.0 reduce-scatter.9.cloned.1.call-start
  535.7 14.6 %fusion.14 = bf16[1,768,3072]{2,1,0:T(8,128)(2,1)} fusion(bf16[2048,768]{1,0:T(8,128)(2,1)S(1)} %bitcast.73, bf16[2048,3072]{1,0:T(8,128)(2,1)} %fusion.6), kind=kOutput, calls=%fused_computation.28 | convolution fusion | flops 9666035712 | bytes 20447232 | tf_op jit(solution)/shard_map/dot_general | solution.py:46
  550.4 0.0 reduce-scatter.11.cloned.1.call-start
  550.4 15.7 %fusion.15 = bf16[1,3072,768]{2,1,0:T(8,128)(2,1)} fusion(bf16[2048,3072]{1,0:T(8,128)(2,1)} %get-tuple-element.28, bf16[2048,768]{1,0:T(8,128)(2,1)} %bitcast.13), kind=kOutput, calls=%fused_computation.29 | convolution fusion | flops 9666035712 | bytes 20447232 | tf_op jit(solution)/shard_map/dot_general | solution.py:46
  566.3 1.8 copy-done.8
  568.1 3.9 convolution_convert_fusion.3.do_ref
  572.0 29.8 %shard_map.162 = bf16[1024,2304]{1,0:T(8,128)(2,1)} custom-call(bf16[1024,2304]{1,0:T(8,128)(2,1)} %get-tuple-element.12.qkv_ref, bf16[1024,768]{1,0:T(8,128)(2,1)} %get-tuple-element.11.ctx_ref, f32[16,1024]{1,0:T(8,128)} %get-tuple-element.13.lse_ref, bf16[1024,768]{1,0:T(8,128)(2,1)} %convolution_convert_fusion.3.do_ref), custom_call_target="tpu_custom_call" | custom-call | tf_op jit(solution)/shard_map/pallas_call | solution.py:180
  601.8 7.7 convolution_convert_fusion.2
  609.5 1.4 copy-done.6
  610.9 9.3 %fusion.37 = (f32[768]{0:T(1024)S(1)}, f32[1024]{0:T(1024)S(1)}, f32[1024]{0:T(1024)S(1)}, f32[1024,768]{1,0:T(8,128)}) fusion(bf16[1024,768]{1,0:T(8,128)(2,1)S(1)} %copy-done.6, f32[1024]{0:T(1024)S(1)} %copy-done.19, f32[1024]{0:T(1024)S(1)} %copy-done.15, f32[768]{0:T(1024)S(1)} %copy-done.17, bf16[1024,2304]{1,0:T(8,128)(2,1)} %shard_map.162, ...), kind=kOutput, calls=%fused_computation.49 | convolution fusion | flops 3630953728 | bytes 12998656 | tf_op jit(solution)/shard_map/dot_general | solution.py:52
  620.2 37.9 %psum.7 = f32[2,768]{1,0:T(2,128)S(1)} all-reduce(f32[2,768]{1,0:T(2,128)S(1)} %pad_maximum_fusion.1), channel_id=1, replica_groups=mesh['dp'=4,'expert'=8] {'dp','expert'}, use_global_device_ids=true, to_apply=%region_17.18 | all-reduce | flops 1536 | bytes 12288 | tf_op jit(solution)/shard_map/psum | solution.py:300
  658.1 0.1 constant_dynamic-slice_fusion
  658.2 0.5 slice_bitcast_fusion
  658.7 4.3 fusion.36
  663.0 1.4 convert_element_type.122
  664.5 16.3 %reduce-scatter.9.cloned.1.call-done = bf16[1,768,768]{2,1,0:T(8,128)(2,1)} async-done(((bf16[1,768,3072]{2,1,0:T(8,128)(2,1)}), bf16[1,768,768]{2,1,0:T(8,128)(2,1)}) %reduce-scatter.9.cloned.1.call-update) | async-done | bytes 1179664 | tf_op jit(solution)/shard_map/reduce_scatter | solution.py:264
  680.8 2.8 convert_element_type.125
  683.7 47.7 %reduce-scatter.11.cloned.1.call-done = bf16[1,768,768]{2,1,0:T(8,128)(2,1)} async-done(((bf16[1,3072,768]{2,1,0:T(8,128)(2,1)}), bf16[1,768,768]{2,1,0:T(8,128)(2,1)}) %reduce-scatter.11.cloned.1.call-update) | async-done | bytes 1179664 | tf_op jit(solution)/shard_map/reduce_scatter | solution.py:267
  731.4 2.8 convert_element_type.128
  734.2 105.7 %reduce-scatter.5.cloned.1.call-done = bf16[24,2304]{1,0:T(8,128)(2,1)} async-done(((bf16[768,2304]{1,0:T(8,128)(2,1)}), bf16[24,2304]{1,0:T(8,128)(2,1)}) %reduce-scatter.5.cloned.1.call-update) | async-done | bytes 110608 | tf_op jit(solution)/shard_map/reduce_scatter | solution.py:294
  839.9 1.6 convert_element_type.120
  (66 shorter events, 0.4 us)
Async XLA Ops:
  7.2 5.4 copy-start
  7.2 14.3 %copy-start.4 = (bf16[1024,768]{1,0:T(8,128)(2,1)S(1)}, bf16[1024,768]{1,0:T(8,128)(2,1)}, u32[]{:S(2)}) copy-start(bf16[1024,768]{1,0:T(8,128)(2,1)} %param.10) | copy-start | bytes 4718596
  7.2 61.8 %all-gather.5.cloned.1.call-start = ((), (), s32[]{:S(2)}) async-start(), calls=%async_computation.8 | async-start | bytes 1419264 | tf_op jit(solution)/shard_map/all_gather | solution.py:195
  10.3 120.8 %all-gather.7.cloned.1.call-start = ((), (), s32[]{:S(2)}) async-start(), calls=%async_computation.9 | async-start | bytes 3649536 | tf_op jit(solution)/shard_map/all_gather | solution.py:194
  11.1 244.3 %all-gather.9.cloned.1.call-start = ((), (), s32[]{:S(2)}) async-start(), calls=%async_computation.10 | async-start | bytes 5898240 | tf_op jit(solution)/shard_map/all_gather | solution.py:231
  21.8 142.4 %copy-start.14 = (f32[1024]{0:T(1024)}, f32[1024]{0:T(1024)S(1)}, u32[]{:S(2)}) copy-start(f32[1024]{0:T(1024)S(1)} %broadcast_multiply_fusion.5) | copy-start | bytes 12292
  22.5 141.8 %copy-start.18 = (f32[1024]{0:T(1024)}, f32[1024]{0:T(1024)S(1)}, u32[]{:S(2)}) copy-start(f32[1024]{0:T(1024)S(1)} %add_rsqrt_fusion.1) | copy-start | bytes 12292
  70.3 94.0 %copy-start.16 = (f32[768]{0:T(1024)}, f32[768]{0:T(1024)S(1)}, u32[]{:S(2)}) copy-start(f32[768]{0:T(1024)S(1)} %get-tuple-element.21) | copy-start | bytes 9220
  131.1 33.1 %copy-start.5 = (bf16[1024,768]{1,0:T(8,128)(2,1)S(1)}, bf16[1024,768]{1,0:T(8,128)(2,1)}, u32[]{:S(2)}) copy-start(bf16[1024,768]{1,0:T(8,128)(2,1)} %param.10) | copy-start | bytes 4718596
  131.1 33.1 %copy-start.13 = (bf16[768,770]{1,0:T(8,128)(2,1)S(1)}, bf16[768,770]{1,0:T(8,128)(2,1)}, u32[]{:S(2)}) copy-start(bf16[768,770]{1,0:T(8,128)(2,1)} %all-gather.5.cloned.1.call-done) | copy-start | bytes 3548164
  167.3 8.2 copy-start.2
  175.5 75.4 %all-to-all-start = ((bf16[8,256,768]{2,1,0:T(8,128)(2,1)}), bf16[8,256,768]{2,1,0:T(8,128)(2,1)S(1)}, u32[]{:S(2)}, u32[]{:S(2)}) async-start(bf16[8,256,768]{2,1,0:T(8,128)(2,1)} %bitcast.71), calls=%async_computation | async-start | bytes 6291456 | tf_op jit(solution)/shard_map/all_to_all | solution.py:223
  179.7 145.9 %all-gather.11.cloned.1.call-start = ((), (), s32[]{:S(2)}) async-start(), calls=%async_computation.11 | async-start | bytes 5898240 | tf_op jit(solution)/shard_map/all_gather | solution.py:232
  250.9 4.5 copy-start.10
  250.9 74.8 %all-to-all-start.2 = ((bf16[8,256,768]{2,1,0:T(8,128)(2,1)}), bf16[8,256,768]{2,1,0:T(8,128)(2,1)}, u32[]{:S(2)}, u32[]{:S(2)}) async-start(bf16[8,256,768]{2,1,0:T(8,128)(2,1)} %bitcast.12), calls=%async_computation.2 | async-start | bytes 6291456 | tf_op jit(solution)/shard_map/all_to_all | solution.py:251
  325.7 30.1 %copy-start.20 = (bf16[1,768,3072]{2,1,0:T(8,128)(2,1)S(1)}, bf16[1,768,3072]{2,1,0:T(8,128)(2,1)}, u32[]{:S(2)}) copy-start(bf16[1,768,3072]{2,1,0:T(8,128)(2,1)} %all-gather.9.cloned.1.call-done) | copy-start | bytes 14155780
  370.3 74.5 %all-to-all-start.3 = ((bf16[8,256,768]{2,1,0:T(8,128)(2,1)}), bf16[8,256,768]{2,1,0:T(8,128)(2,1)S(1)}, u32[]{:S(2)}, u32[]{:S(2)}) async-start(bf16[8,256,768]{2,1,0:T(8,128)(2,1)} %bitcast.75), calls=%async_computation.3 | async-start | bytes 6291456 | tf_op jit(solution)/shard_map/all_to_all | solution.py:271
  444.8 74.6 %all-to-all-start.1 = ((bf16[8,256,768]{2,1,0:T(8,128)(2,1)}), bf16[8,256,768]{2,1,0:T(8,128)(2,1)}, u32[]{:S(2)}, u32[]{:S(2)}) async-start(bf16[8,256,768]{2,1,0:T(8,128)(2,1)} %bitcast.74), calls=%async_computation.1 | async-start | bytes 6291456 | tf_op jit(solution)/shard_map/all_to_all | solution.py:241
  449.2 213.8 %reduce-scatter.7.cloned.1.call-start = ((), (), s32[]{:S(2)}) async-start(), calls=%async_computation.13 | async-start | bytes 1216512 | tf_op jit(solution)/shard_map/reduce_scatter | solution.py:297
  519.4 8.0 copy-start.3
  527.4 5.7 copy-start.12
  531.5 1.6 copy-start.7
  533.1 2.6 copy-start.11
  535.7 145.1 %reduce-scatter.9.cloned.1.call-start = ((), (), s32[]{:S(2)}) async-start(), calls=%async_computation.14 | async-start | bytes 5898240 | tf_op jit(solution)/shard_map/reduce_scatter | solution.py:264
  550.4 181.0 %reduce-scatter.11.cloned.1.call-start = ((), (), s32[]{:S(2)}) async-start(), calls=%async_computation.15 | async-start | bytes 5898240 | tf_op jit(solution)/shard_map/reduce_scatter | solution.py:267
  566.2 1.9 copy-start.8
  566.2 273.7 %reduce-scatter.5.cloned.1.call-start = ((), (), s32[]{:S(2)}) async-start(), calls=%async_computation.12 | async-start | bytes 3649536 | tf_op jit(solution)/shard_map/reduce_scatter | solution.py:294
  572.0 29.8 %copy-start.9 = (bf16[1024,768]{1,0:T(8,128)(2,1)S(1)}, bf16[1024,768]{1,0:T(8,128)(2,1)}, u32[]{:S(2)}) copy-start(bf16[1024,768]{1,0:T(8,128)(2,1)} %fusion.31.act_ref) | copy-start | bytes 4718596
  609.5 1.4 copy-start.6
  609.5 1.4 copy-start.15
  609.5 1.4 copy-start.17
  609.5 1.4 copy-start.19
  663.0 178.5 %copy-start.1 = (s32[50304]{0:T(1024)S(1)}, s32[50304]{0:T(1024)}, u32[]{:S(2)}) copy-start(s32[50304]{0:T(1024)} %param.12) | copy-start | bytes 603652
Sparse Core Ops, SparseCore 0:
  11.6 57.3 all-gather.4
  72.0 59.1 all-gather.6
  132.7 36.2 all-gather.8
  181.8 38.1 all-gather.10
  535.8 95.0 reduce-scatter.6
  633.3 47.4 reduce-scatter.8
  683.5 47.8 reduce-scatter.10
  736.8 103.0 reduce-scatter.4
